TPU v7x, 512 devices: a whole 4x4x16 slice. The times are simulated.
512 devices in a mesh: dp: 32 (over y, x, core), tensor: 16 (over z).
Axes of the slice: x: 4, y: 4, z: 16, core: 2. Of those that a mesh axis runs over, the one named last changes fastest.
Arguments:
- hidden: bfloat16 [24576, 4096], P('dp', 'tensor'), may hold values from -4 to 4
- queries: bfloat16 [24576, 4096], P('dp', 'tensor')
- database: bfloat16 [1024, 128, 896], P('dp', 'tensor'), may hold values from -6 to 6
- w_key: bfloat16 [896, 4096], P(None, 'tensor'), may hold values from -0.1875 to 0.1875
- w_value: bfloat16 [896, 4096], P(None, 'tensor'), may hold values from -0.1875 to 0.1875
- w_out: bfloat16 [4096, 4096], P(None, 'tensor'), may hold values from -0.09375 to 0.09375
- owners: int32 [384, 2], P('dp'), may hold values from 0 to 31, all different within a row; in each aligned block of 12 rows (0 to 11, 12 to 23, ...) at most 2 rows name the same one
- entry_slots: int32 [384, 2], P('dp'), may hold values from 0 to 31
Outputs:
- mixed: bfloat16 [24576, 4096], P('dp', 'tensor')
Inputs may be any that keep to these rules, and one draw needn't show every extreme that they name: Among the spans of one dp index (aligned blocks of 12 rows) no owner is named more than 2 times, a bound that some block reaches; the 2 neighbours of a span have different owners.
All inputs are finite; a program needn't handle non-finite values.
Results may differ from a plain program's by a relative error of at most 0.012.
The roundings to bfloat16 on the way count: a program that leaves them out, or rounds other values in their place, can miss the bound.
Values may be sent and summed in bfloat16 or wider, within the bound.
A program may use at most 64 MiB of HBM per device.

v0:
```python
import math

import jax
import jax.numpy as jnp
from jax import lax
from jax.sharding import PartitionSpec as P

HEAD_DIM = 128


def per_device(hidden, queries, database, w_key, w_value, w_out, owners, entry_slots):
    dp_size = lax.axis_size("dp")
    span_count = owners.shape[0]
    per_span = owners.shape[1]
    capacity = max(2, (per_span * span_count + dp_size - 1) // dp_size)
    wanted = owners.reshape(-1)
    local_slot = entry_slots.reshape(-1)
    requests_here = wanted.shape[0]
    same_owner = wanted[:, None] == wanted[None, :]
    before = jnp.arange(requests_here)[None, :] < jnp.arange(requests_here)[:, None]
    order_in = jnp.sum(jnp.where(same_owner & before, 1, 0), axis=1).astype(jnp.int32)
    position = wanted * capacity + order_in
    placed = position[:, None] == jnp.arange(dp_size * capacity, dtype=jnp.int32)[None, :]
    request_table = jnp.sum(jnp.where(placed, (local_slot + 1)[:, None], 0), axis=0)
    request_table = request_table.reshape(dp_size, capacity)
    incoming = lax.all_to_all(request_table, "dp", split_axis=0, concat_axis=0, tiled=True)
    served_rows = jnp.maximum(incoming - 1, 0).reshape(-1)
    served = jnp.take(database, served_rows, axis=0)
    served = served.reshape(dp_size, capacity, database.shape[1], database.shape[2])
    replies = lax.all_to_all(served, "dp", split_axis=0, concat_axis=0, tiled=True)
    reply_rows = replies.reshape(dp_size * capacity, database.shape[1] * database.shape[2])
    fetched = jnp.dot(
        placed.astype(jnp.bfloat16), reply_rows, preferred_element_type=jnp.float32
    ).astype(jnp.bfloat16)
    fetched = fetched.reshape(requests_here, database.shape[1], database.shape[2])
    proj_weight = jnp.concatenate([w_key, w_value], axis=1)
    piece = lax.all_gather(fetched, "tensor", axis=1, tiled=True)
    flat_piece = piece.reshape(piece.shape[0] * piece.shape[1], piece.shape[2])
    result = jnp.dot(flat_piece, proj_weight, preferred_element_type=jnp.float32).astype(
        jnp.bfloat16
    )
    key_value = result.reshape(piece.shape[0], piece.shape[1], proj_weight.shape[1])
    width = w_key.shape[1]
    heads_here = width // HEAD_DIM
    key_value = key_value.reshape(
        span_count, per_span * key_value.shape[1], 2, heads_here, HEAD_DIM
    )
    key_rows = key_value[:, :, 0]
    value_rows = key_value[:, :, 1]
    span_size = queries.shape[0] // span_count
    query_rows = queries.reshape(span_count, span_size, heads_here, HEAD_DIM)
    score_scale = 1.0 / math.sqrt(HEAD_DIM)
    scores = (
        jnp.einsum("cihd,cjhd->chij", query_rows, key_rows, preferred_element_type=jnp.float32)
        * score_scale
    )
    row_max = jnp.max(scores, axis=-1, keepdims=True)
    weights = jnp.exp(scores - row_max)
    weights = weights / jnp.sum(weights, axis=-1, keepdims=True)
    softmax_low = weights.astype(jnp.bfloat16)
    attended = jnp.einsum(
        "chij,cjhd->cihd", softmax_low, value_rows, preferred_element_type=jnp.float32
    )
    attended = attended.astype(jnp.bfloat16).reshape(queries.shape[0], width)
    gathered = lax.all_gather(attended, "tensor", axis=1, tiled=True)
    projected = jnp.dot(gathered, w_out, preferred_element_type=jnp.float32)
    return (hidden.astype(jnp.float32) + projected).astype(jnp.bfloat16)


def solution(mesh):
    in_specs = (
        P("dp", "tensor"),
        P("dp", "tensor"),
        P("dp", "tensor", None),
        P(None, "tensor"),
        P(None, "tensor"),
        P(None, "tensor"),
        P("dp", None),
        P("dp", None),
    )
    out_specs = P("dp", "tensor")
    return jax.shard_map(
        per_device, mesh=mesh, in_specs=in_specs, out_specs=out_specs, check_vma=False
    )
```

profile of v0, /device:TPU:32, one launch (start us, length us, event | category | flops | bytes accessed | tf_op | source)
XLA Modules:
  0.0 276.5 jit_solution(5320684096094378514)
XLA Ops:
  6.5 0.9 copy.42
  7.5 0.1 reshape.77
  7.5 0.2 select_reduce_fusion.1
  7.7 0.7 broadcast_add_fusion
  8.4 0.1 copy.43
  8.5 0.1 add.43
  8.6 0.1 select_reduce_fusion
  8.7 0.1 all_to_all.9
  8.8 14.5 %all_to_all.14 = s32[32,1,2]{2,1,0:T(1,128)S(1)} all-to-all(s32[32,1,2]{2,1,0:T(1,128)S(1)} %bitcast.54), channel_id=1, replica_groups=mesh['dp'=32,'tensor'=16] {'dp'}, dimensions={0} | all-to-all | bytes 512 | tf_op jit(solution)/shard_map/all_to_all | solution.py:26
  23.3 0.1 copy.45
  23.4 0.1 copy.47
  23.5 0.1 reshape.85
  23.6 0.1 copy.46
  23.7 1.7 gather_fusion
  25.4 0.2 broadcast_select_fusion
  25.6 19.2 %all_to_all.15 = bf16[32,2,8,896]{3,2,1,0:T(8,128)(2,1)S(1)} all-to-all(bf16[32,2,8,896]{3,2,1,0:T(8,128)(2,1)S(1)} %broadcast_select_fusion), channel_id=1, replica_groups=mesh['dp'=32,'tensor'=16] {'dp'}, dimensions={0} | all-to-all | bytes 1835008 | tf_op jit(solution)/shard_map/all_to_all | solution.py:30
  44.8 0.1 copy.54
  45.0 0.3 convolution_convert_fusion
  45.3 0.8 copy.55
  46.2 0.1 reshape.81
  46.3 82.7 %all-gather.3.cloned.1.call-done = bf16[24,128,896]{2,1,0:T(8,128)(2,1)} async-done(((bf16[24,8,896]{2,1,0:T(8,128)(2,1)}), bf16[24,128,896]{2,1,0:T(8,128)(2,1)}) %all-gather.3.cloned.1.call-update) | async-done | bytes 5505040 | tf_op jit(solution)/shard_map/all_gather | solution.py:37
  128.9 7.7 %convolution_convert_fusion.1 = bf16[3072,512]{1,0:T(8,128)(2,1)} fusion(bf16[3072,896]{1,0:T(8,128)(2,1)} %bitcast.55, bf16[896,256]{1,0:T(8,128)(2,1)S(1)} %copy-done.3, bf16[896,256]{1,0:T(8,128)(2,1)} %param.11), kind=kOutput, calls=%fused_computation.3 | convolution fusion | flops 2821980160 | bytes 9568256 | tf_op jit(solution)/shard_map/dot_general | solution.py:39
  136.7 5.5 %reshape_reshape.3 = bf16[12,256,2,2,128]{4,3,2,1,0:T(2,128)(2,1)} reshape(bf16[3072,512]{1,0:T(8,128)(2,1)} %convolution_convert_fusion.1) | data formatting | bytes 6291456 | tf_op jit(solution)/shard_map/reshape;reshape | solution.py:45
  142.2 4.8 %fusion.25 = (bf16[12,256,1,2,128]{4,3,2,1,0:T(2,128)(2,1)S(1)}, bf16[12,256,1,2,128]{4,3,2,1,0:T(2,128)(2,1)}) fusion(bf16[12,256,2,2,128]{4,3,2,1,0:T(2,128)(2,1)} %reshape_reshape.3), kind=kLoop, calls=%fused_computation.38 | loop fusion | bytes 6291456 | tf_op jit(solution)/shard_map/slice | solution.py:48
  147.0 0.7 fusion.5
  147.7 1.1 copy-done.1
  148.9 0.5 fusion.26
  149.4 4.6 %fusion.11 = bf16[12,64,2,128]{3,1,2,0:T(8,128)(2,1)S(1)} fusion(bf16[12,256,1,2,128]{4,3,2,1,0:T(2,128)(2,1)} %get-tuple-element.6, f32[12,2,64]{2,1,0:T(2,128)S(1)} %fusion.26, f32[12,2,256,64]{2,3,1,0:T(8,128)} %copy-done.1), kind=kOutput, calls=%fused_computation.17 | convolution fusion | flops 102041344 | bytes 3545088 | tf_op jit(solution)/shard_map/chij,cjhd->cihd/dot_general | solution.py:61
  154.0 0.4 copy.51
  154.4 0.8 copy.70
  155.3 109.1 %all-gather.5.cloned.1.call-done = bf16[768,4096]{1,0:T(8,128)(2,1)} async-done(((bf16[768,256]{1,0:T(8,128)(2,1)}), bf16[768,4096]{1,0:T(8,128)(2,1)}) %all-gather.5.cloned.1.call-update) | async-done | bytes 6291472 | tf_op jit(solution)/shard_map/all_gather | solution.py:65
  264.3 5.3 %fusion.9 = bf16[768,256]{1,0:T(8,128)(2,1)} fusion(bf16[768,4096]{1,0:T(8,128)(2,1)} %all-gather.5.cloned.1.call-done, bf16[4096,256]{1,0:T(8,128)(2,1)S(1)} %copy-done, bf16[768,256]{1,0:T(8,128)(2,1)S(1)} %copy-done.4), kind=kOutput, calls=%fused_computation.15 | convolution fusion | flops 1611202560 | bytes 9175040 | tf_op jit(solution)/shard_map/dot_general | solution.py:66
  (17 shorter events, 0.1 us)
Async XLA Ops:
  6.5 257.8 %copy-start = (bf16[4096,256]{1,0:T(8,128)(2,1)S(1)}, bf16[4096,256]{1,0:T(8,128)(2,1)}, u32[]{:S(2)}) copy-start(bf16[4096,256]{1,0:T(8,128)(2,1)} %param.13) | copy-start | bytes 6291460
  6.5 122.4 %all-gather.3.cloned.1.call-start = ((), (), s32[]{:S(2)}) async-start(), calls=%async_computation.2 | async-start | bytes 5849088 | tf_op jit(solution)/shard_map/all_gather | solution.py:37
  45.0 1.2 copy-start.2
  45.0 83.9 %copy-start.3 = (bf16[896,256]{1,0:T(8,128)(2,1)S(1)}, bf16[896,256]{1,0:T(8,128)(2,1)}, u32[]{:S(2)}) copy-start(bf16[896,256]{1,0:T(8,128)(2,1)} %param.12) | copy-start | bytes 1376260
  46.1 218.2 %all-gather.5.cloned.1.call-start = ((), (), s32[]{:S(2)}) async-start(), calls=%async_computation.3 | async-start | bytes 6684672 | tf_op jit(solution)/shard_map/all_gather | solution.py:65
  147.7 1.2 copy-start.1
  154.0 110.3 %copy-start.4 = (bf16[768,256]{1,0:T(8,128)(2,1)S(1)}, bf16[768,256]{1,0:T(8,128)(2,1)}, u32[]{:S(2)}) copy-start(bf16[768,256]{1,0:T(8,128)(2,1)} %param.8) | copy-start | bytes 1179652
Sparse Core Ops, SparseCore 0:
  46.2 82.6 all-gather.2
  155.4 108.8 all-gather.4
where the time goes:
time: 277 us; the launch traced here: 276 us
  waiting for transfers between devices  192 us (69%)
  blocking collectives  33.7 us (12%)
  matrix products  18.7 us (7%)
  local copies, waits for them, and re-layouts  17.1 us (6%)
  between operations  13.5 us (5%)
    all_gather x1, waiting for transfers between devices, per_device(): gathered = lax.all_gather(attended, 'tensor', axis=1, tiled=True)  109 us
    all_gather x1, waiting for transfers between devices, per_device(): piece = lax.all_gather(fetched, 'tensor', axis=1, tiled=True)  82.7 us
    all_to_all x1, blocking collectives, per_device(): lax.all_to_all(served, 'dp', split_axis=0, concat_axis=0, tiled=True)  19.2 us
    all_to_all x1, blocking collectives, per_device(): lax.all_to_all(request_table, 'dp', split_axis=0, concat_axis=0, tiled=True)  14.5 us
    dot_general x1, matrix products, per_device(): jnp.dot(flat_piece, proj_weight, preferred_element_type=jnp.float32)  7.74 us
  transfers between devices with their start and end apart: 2, of which 2 were waited for; matrix products, arithmetic and copies ran while one was open for 0% of the time, Pallas kernels for 0%

commit v1 on v0

v1 whole, which is shorter than its diff:
```python
import functools
import math

import jax
import jax.numpy as jnp
from jax import lax
from jax.experimental import pallas as pl
from jax.experimental.pallas import tpu as pltpu
from jax.sharding import PartitionSpec as P

MESH = pl.DeviceIdType.MESH
BF = jnp.bfloat16
F32 = jnp.float32
NP = 12
PIECE = 128


def where_am_i():
    dp = lax.axis_index("dp")
    z = lax.axis_index("tensor")
    y = dp // 8
    x = lax.rem(dp // 2, 4)
    c = lax.rem(dp, 2)
    return dp, z, y, x, c, 2 * y + c


def dp_of(x, j):
    return (j // 2) * 8 + x * 2 + lax.rem(j, 2)


def turn(j, p):
    return lax.rem(p // 4 + j, 4)


def has_span(j, p):
    return turn(j, p) < 3


def slot_of(j, p):
    return (j // 4) * 3 + turn(j, p)


def span_of(j, p):
    return 4 * turn(j, p) + lax.rem(p, 4)


def plane_of(j, k):
    return 4 * lax.rem(k // 4 - j + 8, 4) + lax.rem(k, 4)


def remote(src, dst, ssem, rsem, dp, z):
    return pltpu.make_async_remote_copy(
        src_ref=src, dst_ref=dst, send_sem=ssem, recv_sem=rsem,
        device_id=(dp, z), device_id_type=MESH,
    )


def loop(lo, hi, body):
    def step(i, carry):
        body(i)
        return carry

    lax.fori_loop(lo, hi, step, 0)


def gather_yc(view, here, ssem, rsem, good, half):
    dp, z, y, x, c, j = here

    def at(dy, dc):
        return 2 * lax.rem(y + dy + 4, 4) + lax.rem(c + dc, 2)

    def send(block, part, target, number):
        return remote(view(block, part), view(block, part), ssem.at[number, part],
                      rsem.at[block, part], dp_of(x, target), z)

    up, down, twin, far = at(1, 0), at(-1, 0), at(0, 1), at(2, 0)
    if half is not None:

        @pl.when(good(j))
        def _():
            send(j, half, up, 0).start()
            send(j, half, down, 1).start()
            send(j, half, twin, 2).start()

        return None

    def forward():
        for part in (0, 1):

            @pl.when(good(down))
            def _():
                send(down, part, j, 0).wait_recv()
                if part == 0:
                    send(down, part, up, 6).start()
                send(down, part, twin, 3).start()

            @pl.when(good(up))
            def _():
                send(up, part, j, 0).wait_recv()
                if part == 1:
                    send(up, part, down, 6).start()
                send(up, part, twin, 4).start()

        for part in (0, 1):

            @pl.when(good(far))
            def _():
                send(far, part, j, 0).wait_recv()
                send(far, part, twin, 5).start()

    def finish():
        for part in (0, 1):
            for dy in (0, 1, 3, 2):
                other = at(dy, 1)

                @pl.when(good(other))
                def _():
                    send(other, part, j, 0).wait_recv()

            @pl.when(good(j))
            def _():
                for number in (0, 1, 2):
                    send(j, part, twin, number).wait_send()

            for number, block in ((3, down), (4, up), (5, far)):

                @pl.when(good(block))
                def _():
                    send(block, part, twin, number).wait_send()

        @pl.when(good(down))
        def _():
            send(down, 0, up, 6).wait_send()

        @pl.when(good(up))
        def _():
            send(up, 1, down, 6).wait_send()

    return forward, finish


def fetch_kernel(req_ref, sel_ref, db_ref, q_ref, w_ref, near_ref, q6_ref, wall_ref,
                 qa, rall, served, replies, mine,
                 rs, rr, qs, qr, q2s, q2r, as_, ar, ns, nr, gs, gr, zs, zr, xs, xr, fs, fr, lsem):
    here = where_am_i()
    dp, z, y, x, c, j = here
    barrier = pltpu.get_barrier_semaphore()

    def greet(i):
        pl.semaphore_signal(barrier, inc=1, device_id=(lax.rem(dp + i, 32), z), device_id_type=MESH)

    def greet_z(i):
        pl.semaphore_signal(barrier, inc=1, device_id=(dp, lax.rem(z + i, 16)), device_id_type=MESH)

    loop(1, 32, greet)
    loop(1, 16, greet_z)
    pl.semaphore_wait(barrier, 46)

    def req_copy(source, target):
        return remote(req_ref, rall.at[source], rs.at[target], rr.at[source], target, z)

    loop(1, 32, lambda i: req_copy(dp, lax.rem(dp + i, 32)).start())

    d = lax.rem(z - j + 16, 16)
    e, s = lax.rem(d, 8), d // 8
    right, left = lax.rem(z + 1, 16), lax.rem(z + 15, 16)
    xright, xleft = lax.rem(x + 1, 4), lax.rem(x + 3, 4)

    def wz(h, i, to, way):
        return remote(wall_ref.at[h, x, i], wall_ref.at[h, x, i], zs.at[way, i], zr.at[h, i], dp, to)

    def wx(h, i, way):
        return remote(wall_ref.at[h, x, i], wall_ref.at[h, x, i], xs.at[way, h, i], xr.at[way, h, i],
                      dp_of(xright if way == 0 else xleft, j), z)

    def wx_in(h, i, way):
        chunk = xleft if way == 0 else xright
        return remote(wall_ref.at[h, chunk, i], wall_ref.at[h, chunk, i], fs.at[h, i], xr.at[way, h, i],
                      dp_of(xright, j), z)

    def wf(h, i, way):
        chunk = xleft if way == 0 else xright
        return remote(wall_ref.at[h, chunk, i], wall_ref.at[h, chunk, i], fs.at[h, i], fr.at[h, i],
                      dp_of(xright if way == 0 else xleft, j), z)

    @pl.when(e == 0)
    def _():
        own = pltpu.make_async_copy(w_ref, wall_ref.at[s, x], lsem.at[0])
        own.start()
        own.wait()

        def inject(i):
            wz(s, i, right, 0).start()
            wz(s, i, left, 1).start()

        loop(0, NP, inject)

    def q_copy(k):
        p = plane_of(j, k)
        return p, remote(q_ref.at[k], qa.at[z // 8, lax.rem(z, 8)], qs.at[k],
                         qr.at[z], dp, p)

    def q_local(k):
        return pltpu.make_async_copy(q_ref.at[k], qa.at[z // 8, lax.rem(z, 8)], lsem.at[1])

    def q_send(k):
        p, copy = q_copy(k)

        @pl.when(p == z)
        def _():
            q_local(k).start()

        @pl.when(p != z)
        def _():
            copy.start()

    loop(0, 12, q_send)

    def slot(t):
        ia = t - e
        ib = t - 8 + e

        @pl.when((ia >= 0) & (ia < NP))
        def _():
            @pl.when(e > 0)
            def _():
                wz(s, ia, z, 0).wait_recv()
                wz(s, ia, right, 0).start()

            wx(s, ia, 0).start()
            wx(s, ia, 1).start()

        @pl.when((ib >= 0) & (ib < NP))
        def _():
            wz(1 - s, ib, z, 0).wait_recv()

            @pl.when(e >= 2)
            def _():
                wz(1 - s, ib, left, 1).start()

            wx(1 - s, ib, 0).start()
            wx(1 - s, ib, 1).start()

        for h, i in ((s, ia - 2), (1 - s, ib - 2)):

            @pl.when((i >= 0) & (i < NP))
            def _():
                wx_in(h, i, 0).wait_recv()
                wx_in(h, i, 1).wait_recv()

                @pl.when(lax.rem(i, 2) == 0)
                def _():
                    wf(h, i, 0).start()

                @pl.when(lax.rem(i, 2) == 1)
                def _():
                    wf(h, i, 1).start()

    rall[dp] = req_ref[...]
    loop(1, 32, lambda i: req_copy(lax.rem(dp + i, 32), dp).wait_recv())
    table = rall[:, 0, :].astype(F32).astype(BF)
    expand = (lax.broadcasted_iota(jnp.int32, (512, 32), 0) // 16
              == lax.broadcasted_iota(jnp.int32, (512, 32), 1)).astype(F32).astype(BF)
    spread = jnp.dot(expand, table, preferred_element_type=F32)
    row = lax.broadcasted_iota(jnp.int32, (512, 128), 0)
    lane = lax.broadcasted_iota(jnp.int32, (512, 128), 1)
    entry = jnp.sum(jnp.where(lane == 2 * dp + (row // 8) % 2, spread, 0.0), axis=1, keepdims=True)
    row = lax.broadcasted_iota(jnp.int32, (512, 256), 0)
    column = lax.broadcasted_iota(jnp.int32, (512, 256), 1)
    hot = ((column // 8 + 1).astype(F32) == entry) & (column % 8 == row % 8)
    picked = jnp.dot(hot.astype(F32).astype(BF), db_ref[...], preferred_element_type=F32)
    served[...] = picked.astype(BF).reshape(32, 16, 896)

    def reply(source, target):
        return remote(served.at[target], replies.at[source], as_.at[target], ar.at[source], target, z)

    loop(1, 32, lambda i: reply(dp, lax.rem(dp + i, 32)).start())
    loop(0, 5, slot)
    replies[dp] = served[dp]
    loop(1, 32, lambda i: reply(lax.rem(dp + i, 32), dp).wait_recv())
    got = jnp.dot(sel_ref[...], replies[...].reshape(512, 896), preferred_element_type=F32)
    mine[...] = got.astype(BF).reshape(12, 16, 896)

    def n_copy(k):
        p = plane_of(j, k)
        return p, remote(mine.at[k], near_ref.at[slot_of(j, p), z], ns.at[k], nr.at[z], dp, p)

    def n_local(k):
        return pltpu.make_async_copy(mine.at[k], near_ref.at[slot_of(j, z), z], lsem.at[2])

    def n_send(k):
        p, copy = n_copy(k)

        @pl.when(p == z)
        def _():
            n_local(k).start()

        @pl.when(p != z)
        def _():
            copy.start()

    loop(0, 12, n_send)
    loop(5, 9, slot)

    def q2(source, target):
        return remote(qa.at[:, target], q6_ref.at[slot_of(source, z)], q2s.at[target], q2r.at[source],
                      dp_of(x, target), z)

    def q2_local():
        return pltpu.make_async_copy(qa.at[:, j], q6_ref.at[slot_of(j, z)], lsem.at[3])

    @pl.when(has_span(j, z))
    def _():
        q_local(0).wait()
        loop(1, 16, lambda i: remote(q_ref.at[0], qa.at[0, 0], qs.at[0], qr.at[lax.rem(z + i, 16)],
                                     dp, z).wait_recv())
        q2_local().start()
        loop(1, 8, lambda i: q2(j, lax.rem(j + i, 8)).start())

    loop(9, 11, slot)

    def view(block, part):
        return near_ref.at[slot_of(block, z), pl.ds(part * 8, 8)]

    def good(block):
        return has_span(block, z)

    @pl.when(good(j))
    def _():
        n_local(0).wait()
        loop(1, 16, lambda i: remote(mine.at[0], near_ref.at[0, 0], ns.at[0], nr.at[lax.rem(z + i, 16)],
                                     dp, z).wait_recv())

    for part in (0, 1):
        gather_yc(view, here, gs, gr, good, part)
    loop(11, 13, slot)
    forward, finish = gather_yc(view, here, gs, gr, good, None)
    forward()
    loop(13, 22, slot)

    finish()

    @pl.when(has_span(j, z))
    def _():
        q2_local().wait()
        loop(1, 8, lambda i: q2(j, lax.rem(j + i, 8)).wait_send())

    def q2_wait(i):
        other = lax.rem(j + i, 8)

        @pl.when(has_span(other, z))
        def _():
            q2(other, j).wait_recv()

    loop(1, 8, q2_wait)

    def sent(k):
        p, copy = n_copy(k)
        _, copy_q = q_copy(k)

        @pl.when(p != z)
        def _():
            copy.wait_send()
            copy_q.wait_send()

    loop(0, 12, sent)

    def sent_dp(i):
        other = lax.rem(dp + i, 32)
        req_copy(dp, other).wait_send()
        reply(dp, other).wait_send()

    loop(1, 32, sent_dp)

    def sent_w(i):
        @pl.when(e >= 0)
        def _():
            wz(s, i, right, 0).wait_send()

        @pl.when(e == 0)
        def _():
            wz(s, i, left, 1).wait_send()

        @pl.when(e >= 2)
        def _():
            wz(1 - s, i, left, 1).wait_send()

        for h in (0, 1):
            wx(h, i, 0).wait_send()
            wx(h, i, 1).wait_send()
            wf(h, i, 0).wait_send()
            wf(h, i, 0).wait_recv()

    loop(0, NP, sent_w)


def attend_kernel(near_ref, q_ref, wall_ref, hid_ref, out_ref,
                  near, wk, wv, wo, att, acc, res, ob, fb,
                  ls, gs, gr, bs, br, cs, cr, lsem):
    here = where_am_i()
    dp, z, y, x, c, j = here
    loads = []

    def load(src, dst, number):
        copy = pltpu.make_async_copy(src, dst, ls.at[number])
        copy.start()
        loads.append(copy)

    for h in (0, 1):
        for chunk in range(4):
            load(wall_ref.at[h, chunk, pl.ds(0, 224)], wk.at[h, pl.ds(224 * chunk, 224)], 16 * h + 4 * chunk)
            load(wall_ref.at[h, chunk, pl.ds(224, 224)], wv.at[h, pl.ds(224 * chunk, 224)],
                 16 * h + 4 * chunk + 1)
    load(near_ref, near, 32)
    first = len(loads)
    for h in (0, 1):
        for chunk in range(4):
            load(wall_ref.at[h, chunk, pl.ds(512, 1024)], wo.at[h, pl.ds(1024 * chunk, 1024)],
                 16 * h + 4 * chunk + 2)

    barrier = pltpu.get_barrier_semaphore()
    loop(1, 8, lambda i: pl.semaphore_signal(
        barrier, inc=1, device_id=(dp_of(x, lax.rem(j + i, 8)), z), device_id_type=MESH))
    loop(1, 16, lambda i: pl.semaphore_signal(
        barrier, inc=1, device_id=(dp, lax.rem(z + i, 16)), device_id_type=MESH))
    pl.semaphore_wait(barrier, 22)
    for copy in loads[:first]:
        copy.wait()

    scale = 1.0 / math.sqrt(128)

    def span(n):
        rows = near[n]
        for h in (0, 1):
            keys = jnp.dot(rows, wk[h], preferred_element_type=F32).astype(BF)
            values = jnp.dot(rows, wv[h], preferred_element_type=F32).astype(BF)
            for m in (0, 1):
                cut = slice(128 * m, 128 * m + 128)
                scores = lax.dot_general(q_ref[n, h, :, cut], keys[:, cut], (((1,), (1,)), ((), ())),
                                         preferred_element_type=F32) * scale
                w = jnp.exp(scores - jnp.max(scores, axis=-1, keepdims=True))
                w = w / jnp.sum(w, axis=-1, keepdims=True)
                o = jnp.dot(w.astype(BF), values[:, cut], preferred_element_type=F32)
                att[j, n, :, 256 * h + 128 * m:256 * h + 128 * m + 128] = o.astype(BF)

    def view(block, part):
        return att.at[block, pl.ds(3 * part, 3)]

    def good(block):
        return block >= 0

    for part in (0, 1):
        loop(3 * part, 3 * part + 3, span)
        gather_yc(view, here, gs, gr, good, part)
    forward, finish = gather_yc(view, here, gs, gr, good, None)
    forward()
    finish()
    for copy in loads[first:]:
        copy.wait()

    acc[...] = jnp.zeros_like(acc)

    def project(b):
        rows = att[b].reshape(384, 512)
        for g in (0, 1):
            total = acc[g]
            for h in (0, 1):
                w = wo[g, pl.ds(pl.multiple_of((b + 8 * h) * 256, 256), 256), :]
                total = total + jnp.dot(rows[:, 256 * h:256 * h + 256], w, preferred_element_type=F32)
            acc[g] = total

    loop(0, 8, project)
    for g in (0, 1):
        res[:, g] = acc[g].astype(BF).reshape(6, 64, 256)

    def b_copy(source, target):
        return remote(res.at[slot_of(target, z)], ob.at[source], bs.at[target], br.at[source],
                      dp_of(x, target), z)

    def b_send(i):
        other = lax.rem(j + i, 8)

        @pl.when(has_span(other, z))
        def _():
            b_copy(j, other).start()

    loop(1, 8, b_send)

    def c_copy(source, h, k):
        to = source + 8 * h
        return to, remote(ob.at[source, h], fb.at[k], cs.at[to], cr.at[k], dp, to)

    def c_local(source, h, k):
        return pltpu.make_async_copy(ob.at[source, h], fb.at[k], lsem.at[0])

    def c_send(source):
        for h in (0, 1):
            to, copy = c_copy(source, h, span_of(j, z))

            @pl.when(to == z)
            def _():
                c_local(source, h, span_of(j, z)).start()

            @pl.when(to != z)
            def _():
                copy.start()

    @pl.when(has_span(j, z))
    def _():
        ob[j] = res[slot_of(j, z)]
        c_send(j)

        def relay(i):
            other = lax.rem(j + i, 8)
            b_copy(other, j).wait_recv()
            c_send(other)

        loop(1, 8, relay)
        c_local(0, 0, 0).wait()

    def land(k):
        @pl.when(plane_of(j, k) != z)
        def _():
            remote(ob.at[0, 0], fb.at[k], cs.at[0], cr.at[k], dp, z).wait_recv()

        out_ref[k] = (hid_ref[k].astype(F32) + fb[k].astype(F32)).astype(BF)

    loop(0, 12, land)

    def b_sent(i):
        other = lax.rem(j + i, 8)

        @pl.when(has_span(other, z))
        def _():
            b_copy(j, other).wait_send()

    loop(1, 8, b_sent)

    @pl.when(has_span(j, z))
    def _():
        def c_sent(i):
            to = lax.rem(z + i, 16)
            remote(ob.at[0, 0], fb.at[0], cs.at[to], cr.at[0], dp, to).wait_send()

        loop(1, 16, c_sent)


def fetch(requests, sel, db, queries, weights):
    dma = pltpu.SemaphoreType.DMA
    any_ = pl.BlockSpec(memory_space=pl.ANY)
    vmem = pl.BlockSpec(memory_space=pltpu.VMEM)
    return pl.pallas_call(
        fetch_kernel,
        name="fetch",
        out_shape=(
            jax.ShapeDtypeStruct((6, 16, 16, 896), BF),
            jax.ShapeDtypeStruct((6, 2, 64, 256), BF),
            jax.ShapeDtypeStruct((2, 4, NP, PIECE, 256), BF),
        ),
        in_specs=[vmem, vmem, vmem, any_, any_],
        out_specs=(any_, any_, any_),
        scratch_shapes=[
            pltpu.VMEM((2, 8, 64, 256), BF),
            pltpu.VMEM((32, 8, 128), jnp.int32),
            pltpu.VMEM((32, 16, 896), BF),
            pltpu.VMEM((32, 16, 896), BF),
            pltpu.VMEM((12, 16, 896), BF),
            dma((32,)), dma((32,)),
            dma((12,)), dma((16,)),
            dma((8,)), dma((8,)),
            dma((32,)), dma((32,)),
            dma((12,)), dma((16,)),
            dma((7, 2)), dma((8, 2)),
            dma((2, NP)), dma((2, NP)),
            dma((2, 2, NP)), dma((2, 2, NP)),
            dma((2, NP)), dma((2, NP)),
            dma((4,)),
        ],
        compiler_params=pltpu.CompilerParams(
            collective_id=0, has_side_effects=True, vmem_limit_bytes=32 * 2**20
        ),
    )(requests, sel, db, queries, weights)


def attend(near, q6, wall, hidden):
    dma = pltpu.SemaphoreType.DMA
    any_ = pl.BlockSpec(memory_space=pl.ANY)
    vmem = pl.BlockSpec(memory_space=pltpu.VMEM)
    return pl.pallas_call(
        attend_kernel,
        name="attend",
        out_shape=jax.ShapeDtypeStruct((12, 64, 256), BF),
        in_specs=[any_, vmem, any_, vmem],
        out_specs=vmem,
        scratch_shapes=[
            pltpu.VMEM((6, 256, 896), BF),
            pltpu.VMEM((2, 896, 256), BF),
            pltpu.VMEM((2, 896, 256), BF),
            pltpu.VMEM((2, 4096, 256), BF),
            pltpu.VMEM((8, 6, 64, 512), BF),
            pltpu.VMEM((2, 384, 256), F32),
            pltpu.VMEM((6, 2, 64, 256), BF),
            pltpu.VMEM((8, 2, 64, 256), BF),
            pltpu.VMEM((12, 64, 256), BF),
            dma((33,)),
            dma((7, 2)), dma((8, 2)),
            dma((8,)), dma((8,)),
            dma((16,)), dma((12,)),
            dma((1,)),
        ],
        compiler_params=pltpu.CompilerParams(
            collective_id=1, has_side_effects=True, vmem_limit_bytes=40 * 2**20
        ),
    )(near, q6, wall, hidden)


def per_device(hidden, queries, database, w_key, w_value, w_out, owners, entry_slots):
    x = lax.rem(lax.axis_index("dp") // 2, 4)
    wanted = owners.reshape(-1)
    slots = entry_slots.reshape(-1)
    number = jnp.arange(24, dtype=jnp.int32)
    same = (wanted[:, None] == wanted[None, :]) & (number[None, :] < number[:, None])
    order = jnp.sum(same.astype(jnp.int32), axis=1)
    position = wanted * 2 + order
    placed = position[:, None] == jnp.arange(128, dtype=jnp.int32)[None, :]
    requests = jnp.sum(jnp.where(placed, (slots + 1)[:, None], 0), axis=0)
    requests = jnp.broadcast_to(requests[None, :], (8, 128))
    token = jnp.arange(8, dtype=jnp.int32)
    source = (position[:, None] * 8 + token[None, :]).reshape(192, 1)
    sel = (source == jnp.arange(512, dtype=jnp.int32)[None, :]).astype(BF)
    take = lambda w, n: lax.dynamic_slice(w, (x * n, 0), (n, 256))
    weights = jnp.concatenate(
        [take(w_key, 224), take(w_value, 224), jnp.zeros((64, 256), BF), take(w_out, 1024)], axis=0
    )
    near, q6, wall = fetch(
        requests, sel, database.reshape(256, 896), queries.reshape(12, 64, 256),
        weights.reshape(NP, PIECE, 256),
    )
    mixed = attend(
        near.reshape(6, 256, 896), q6, wall.reshape(2, 4, NP * PIECE, 256), hidden.reshape(12, 64, 256)
    )
    return mixed.reshape(768, 256)


def solution(mesh):
    in_specs = (
        P("dp", "tensor"),
        P("dp", "tensor"),
        P("dp", "tensor", None),
        P(None, "tensor"),
        P(None, "tensor"),
        P(None, "tensor"),
        P("dp", None),
        P("dp", None),
    )
    return jax.shard_map(
        per_device, mesh=mesh, in_specs=in_specs, out_specs=P("dp", "tensor"), check_vma=False
    )
```

time: 277 us -> 201 us (0.73)
  the two profiles are of different devices: /device:TPU:32 before, /device:TPU:79 now
where the time goes in v1:
time: 201 us
  Pallas kernels  196 us (98%)
  local copies, waits for them, and re-layouts  3.08 us (2%)
    pallas_call x1, Pallas kernels, fetch(): pl.pallas_call(fetch_kernel, name='fetch', out_shape=(jax.ShapeDtypeStruc...  111 us
    pallas_call x1, Pallas kernels, attend(): pl.pallas_call(attend_kernel, name='attend', out_shape=jax.ShapeDtypeStru...  84.9 us

profile of v1, /device:TPU:79, one launch (start us, length us, event | category | flops | bytes accessed | tf_op | source)
XLA Modules:
  0.0 201.0 jit_solution(2461364629425264105)
XLA Ops:
  0.0 0.0 copy-start
  0.0 0.8 broadcast_add_fusion
  0.8 0.1 pad.2.clone
  0.9 0.1 copy.14
  1.0 0.1 add.50
  1.1 0.8 copy.13
  1.9 0.1 reshape.65
  2.0 0.2 convert_reduce_fusion
  2.1 0.1 select_reduce_fusion
  2.2 0.1 iota_add_fusion
  2.3 0.1 add.54
  2.4 0.1 fusion.sel_ref
  2.5 0.0 copy-start.1
  2.5 0.0 copy-start.3
  2.6 1.0 constant_dynamic-slice_fusion
  3.6 0.0 copy-done
  3.7 0.0 copy-start.2
  3.7 0.3 pad_maximum_fusion
  4.0 0.0 copy-done.1
  4.0 0.0 copy-done.3
  4.0 111.4 %fetch.1 = (bf16[6,16,16,896]{3,2,1,0:T(8,128)(2,1)S(1)}, bf16[6,2,64,256]{3,2,1,0:T(8,128)(2,1)S(1)}, bf16[2,4,12,128,256]{4,3,2,1,0:T(8,128)(2,1)S(1)}) custom-call(s32[8,128]{1,0:T(8,128)S(1)} %broadcast_in_dim.18.req_ref, bf16[192,512]{1,0:T(8,128)(2,1)S(1)} %fusion.sel_ref, bf16[256,896]{1,0:T(8,128)(2,1)S(1)} %bitcast.11, ...), custom_call_target="tpu_custom_call" | custom-call | tf_op jit(solution)/shard_map/fetch/pallas_call | solution.py:552
  115.4 0.0 copy-done.2
  115.4 84.9 %attend.1 = bf16[12,64,256]{2,1,0:T(8,128)(2,1)S(1)} custom-call(bf16[6,256,896]{2,1,0:T(8,128)(2,1)S(1)} %bitcast.9, bf16[6,2,64,256]{3,2,1,0:T(8,128)(2,1)S(1)} %get-tuple-element.9.q_ref, bf16[2,4,1536,256]{3,2,1,0:T(8,128)(2,1)S(1)} %bitcast.7, bf16[12,64,256]{2,1,0:T(8,128)(2,1)S(1)} %bitcast.12), custom_call_target="tpu_custom_call" | custom-call | tf_op jit(solution)/shard_map/attend/pallas_call | solution.py:589
  200.3 0.7 copy.16
  (4 shorter events, 0.1 us)
Async XLA Ops:
  0.0 3.6 %copy-start = (bf16[4096,256]{1,0:T(8,128)(2,1)S(1)}, bf16[4096,256]{1,0:T(8,128)(2,1)}, u32[]{:S(2)}) copy-start(bf16[4096,256]{1,0:T(8,128)(2,1)} %param.13) | copy-start | bytes 6291460
  2.5 1.4 copy-start.1
  2.5 1.4 copy-start.3
  3.7 111.7 %copy-start.2 = (bf16[768,256]{1,0:T(8,128)(2,1)S(1)}, bf16[768,256]{1,0:T(8,128)(2,1)}, u32[]{:S(2)}) copy-start(bf16[768,256]{1,0:T(8,128)(2,1)} %param.8) | copy-start | bytes 1179652

commit v2 on v1

v2 whole, which is shorter than its diff:
```python
import functools
import math

import jax
import jax.numpy as jnp
from jax import lax
from jax.experimental import pallas as pl
from jax.experimental.pallas import tpu as pltpu
from jax.sharding import PartitionSpec as P

MESH = pl.DeviceIdType.MESH
BF = jnp.bfloat16
F32 = jnp.float32
NP = 12
NKV = 4
PIECE = 128
SKEW = 1
LAG = 2
LAST = NP + 8 * SKEW + LAG
PACE = dict(ask=2, fetch=4, move=4, near=2, near_step=1, span=1, att_step=1)


def where_am_i():
    dp = lax.axis_index("dp")
    z = lax.axis_index("tensor")
    y = dp // 8
    x = lax.rem(dp // 2, 4)
    c = lax.rem(dp, 2)
    return dp, z, y, x, c, 2 * y + c


def dp_of(x, j):
    return (j // 2) * 8 + x * 2 + lax.rem(j, 2)


def turn(j, p):
    return lax.rem(p // 4 + j, 4)


def has_span(j, p):
    return turn(j, p) < 3


def slot_of(j, p):
    return (j // 4) * 3 + turn(j, p)


def span_of(j, p):
    return 4 * turn(j, p) + lax.rem(p, 4)


def plane_of(j, k):
    return 4 * lax.rem(k // 4 - j + 8, 4) + lax.rem(k, 4)


def remote(src, dst, ssem, rsem, dp, z):
    return pltpu.make_async_remote_copy(
        src_ref=src, dst_ref=dst, send_sem=ssem, recv_sem=rsem,
        device_id=(dp, z), device_id_type=MESH,
    )


def loop(lo, hi, body):
    def step(i, carry):
        body(i)
        return carry

    lax.fori_loop(lo, hi, step, 0)


def gather_yc(view, here, ssem, rsem, good, half, between=None):
    dp, z, y, x, c, j = here

    def at(dy, dc):
        return 2 * lax.rem(y + dy + 4, 4) + lax.rem(c + dc, 2)

    def send(block, part, target, number):
        return remote(view(block, part), view(block, part), ssem.at[number, part],
                      rsem.at[block, part], dp_of(x, target), z)

    up, down, twin, far = at(1, 0), at(-1, 0), at(0, 1), at(2, 0)
    if half is not None:

        @pl.when(good(j))
        def _():
            send(j, half, up, 0).start()
            send(j, half, down, 1).start()
            send(j, half, twin, 2).start()

        return None

    def forward():
        for part in (0, 1):

            @pl.when(good(down))
            def _():
                send(down, part, j, 0).wait_recv()
                if part == 0:
                    send(down, part, up, 6).start()
                send(down, part, twin, 3).start()

            @pl.when(good(up))
            def _():
                send(up, part, j, 0).wait_recv()
                if part == 1:
                    send(up, part, down, 6).start()
                send(up, part, twin, 4).start()

            between()

        for part in (0, 1):

            @pl.when(good(far))
            def _():
                send(far, part, j, 0).wait_recv()
                send(far, part, twin, 5).start()

            between()

    def finish():
        for part in (0, 1):
            for dy in (0, 1, 3, 2):
                other = at(dy, 1)

                @pl.when(good(other))
                def _():
                    send(other, part, j, 0).wait_recv()

            @pl.when(good(j))
            def _():
                for number in (0, 1, 2):
                    send(j, part, twin, number).wait_send()

            for number, block in ((3, down), (4, up), (5, far)):

                @pl.when(good(block))
                def _():
                    send(block, part, twin, number).wait_send()

        @pl.when(good(down))
        def _():
            send(down, 0, up, 6).wait_send()

        @pl.when(good(up))
        def _():
            send(up, 1, down, 6).wait_send()

    return forward, finish


def layer_kernel(own_ref, ent_ref, db_hbm, q_ref, wk_ref, wv_ref, wo_ref, hid_hbm, out_ref,
                 db_ref, hid_ref, req_ref, qa, q6, rall, served, replies, mine, near, wall, att, acc, res, ob, fb,
                 rs, rr, qs, qr, q2s, q2r, as_, ar, ns, nr, gs, gr,
                 wl, zs, zr, xs, xr, fs, fr, ts, tr, bs, br, cs, cr, lsem, load):
    here = where_am_i()
    dp, z, y, x, c, j = here
    d = lax.rem(z - j + 16, 16)
    e, s = lax.rem(d, 8), d // 8
    right, left = lax.rem(z + 1, 16), lax.rem(z + 15, 16)
    xright, xleft = lax.rem(x + 1, 4), lax.rem(x + 3, 4)

    def piece(h, i, chunk):
        return wall.at[h, pl.ds(pl.multiple_of((4 * i + chunk) * PIECE, PIECE), PIECE)]

    load_db = pltpu.make_async_copy(db_hbm, db_ref, load.at[0])
    load_hid = pltpu.make_async_copy(hid_hbm, hid_ref, load.at[1])
    load_db.start()

    def own_rows(ref, g):
        return ref.at[pl.ds(pl.multiple_of(g * PIECE, PIECE), PIECE)]

    def own(i, ref, g):
        return pltpu.make_async_copy(own_rows(ref, g), piece(s, i, x), wl.at[i])

    @pl.when(e == 0)
    def _():
        for i in range(NKV):
            g = 4 * i + x

            @pl.when(g < 7)
            def _():
                own(i, wk_ref, jnp.minimum(g, 6)).start()

            @pl.when(g >= 7)
            def _():
                own(i, wv_ref, jnp.clip(g - 7, 0, 6)).start()

        for i in range(NKV, NP):
            own(i, wo_ref, 4 * (i - NKV) + x).start()

    load_hid.start()
    barrier = pltpu.get_barrier_semaphore()

    def greet(i):
        pl.semaphore_signal(barrier, inc=1, device_id=(lax.rem(dp + i, 32), z), device_id_type=MESH)

    def greet_z(i):
        pl.semaphore_signal(barrier, inc=1, device_id=(dp, lax.rem(z + i, 16)), device_id_type=MESH)

    loop(1, 32, greet)
    loop(1, 16, greet_z)
    pl.semaphore_wait(barrier, 46)

    number = lax.broadcasted_iota(jnp.int32, (24, 12), 0)
    lane = lax.broadcasted_iota(jnp.int32, (24, 12), 1)

    def column(ref):
        both = jnp.where(number < 12, ref[0:1, :], ref[1:2, :])
        return jnp.sum(jnp.where(lane == number % 12, both, 0), axis=1, keepdims=True)

    wanted = column(own_ref)
    order = jnp.zeros((24, 1), jnp.int32)
    for n in (0, 1):
        earlier = (own_ref[n:n + 1, :] == wanted) & (lane + 12 * n < number)
        order = order + jnp.sum(earlier.astype(jnp.int32), axis=1, keepdims=True)
    placed = (2 * wanted + order) == lax.broadcasted_iota(jnp.int32, (24, 128), 1)
    row = jnp.sum(jnp.where(placed, column(ent_ref) + 1, 0), axis=0, keepdims=True)
    req_ref[...] = jnp.broadcast_to(row, (8, 128))

    def req_copy(source, target):
        return remote(req_ref, rall.at[source], rs.at[target], rr.at[source], target, z)

    loop(1, 32, lambda i: req_copy(dp, lax.rem(dp + i, 32)).start())

    def wz(h, i, to, way):
        return remote(piece(h, i, x), piece(h, i, x), zs.at[way, i], zr.at[h, i], dp, to)

    def wx(h, i, way):
        return remote(piece(h, i, x), piece(h, i, x), xs.at[way, h, i], xr.at[way, h, i],
                      dp_of(xright if way == 0 else xleft, j), z)

    def wx_in(h, i, way):
        chunk = xleft if way == 0 else xright
        return remote(piece(h, i, chunk), piece(h, i, chunk), fs.at[h, i], xr.at[way, h, i],
                      dp_of(xright, j), z)

    def wf(h, i, way):
        chunk = xleft if way == 0 else xright
        return remote(piece(h, i, chunk), piece(h, i, chunk), fs.at[h, i], fr.at[h, i],
                      dp_of(xright if way == 0 else xleft, j), z)

    def inject(lo, hi):
        @pl.when(e == 0)
        def _():
            def one(i):
                own(i, wo_ref, 0).wait()
                wz(s, i, right, 0).start()
                wz(s, i, left, 1).start()

            loop(lo, hi, one)

    inject(0, NP)

    def q_copy(k):
        p = plane_of(j, k)
        return p, remote(q_ref.at[k], qa.at[z // 8, lax.rem(z, 8)], qs.at[k],
                         qr.at[z], dp, p)

    def q_local(k):
        return pltpu.make_async_copy(q_ref.at[k], qa.at[z // 8, lax.rem(z, 8)], lsem.at[1])

    def q_send(k):
        p, copy = q_copy(k)

        @pl.when(p == z)
        def _():
            q_local(k).start()

        @pl.when(p != z)
        def _():
            copy.start()

    loop(0, 12, q_send)

    def slot(t):
        ia = t - SKEW * e
        ib = t - SKEW * (8 - e)

        @pl.when((ia >= 0) & (ia < NP))
        def _():
            @pl.when(e > 0)
            def _():
                wz(s, ia, z, 0).wait_recv()
                wz(s, ia, right, 0).start()

            wx(s, ia, 0).start()
            wx(s, ia, 1).start()

        @pl.when((ib >= 0) & (ib < NP))
        def _():
            wz(1 - s, ib, z, 0).wait_recv()

            @pl.when(e >= 2)
            def _():
                wz(1 - s, ib, left, 1).start()

            wx(1 - s, ib, 0).start()
            wx(1 - s, ib, 1).start()

        for h, i in ((s, ia - LAG), (1 - s, ib - LAG)):

            @pl.when((i >= 0) & (i < NP))
            def _():
                wx_in(h, i, 0).wait_recv()
                wx_in(h, i, 1).wait_recv()

                @pl.when(lax.rem(i, 2) == 0)
                def _():
                    wf(h, i, 0).start()

                @pl.when(lax.rem(i, 2) == 1)
                def _():
                    wf(h, i, 1).start()

    done = [0]

    def slots(count):
        upto = min(done[0] + count, LAST)
        if upto > done[0]:
            loop(done[0], upto, slot)
        done[0] = upto

    slots(PACE["ask"])

    rall[dp] = req_ref[...]
    loop(1, 32, lambda i: req_copy(lax.rem(dp + i, 32), dp).wait_recv())
    load_db.wait()
    table = rall[:, 0, :].astype(F32).astype(BF)
    expand = (lax.broadcasted_iota(jnp.int32, (512, 32), 0) // 16
              == lax.broadcasted_iota(jnp.int32, (512, 32), 1)).astype(F32).astype(BF)
    spread = jnp.dot(expand, table, preferred_element_type=F32)
    row = lax.broadcasted_iota(jnp.int32, (512, 128), 0)
    lane = lax.broadcasted_iota(jnp.int32, (512, 128), 1)
    entry = jnp.sum(jnp.where(lane == 2 * dp + (row // 8) % 2, spread, 0.0), axis=1, keepdims=True)
    row = lax.broadcasted_iota(jnp.int32, (512, 256), 0)
    column = lax.broadcasted_iota(jnp.int32, (512, 256), 1)
    hot = ((column // 8 + 1).astype(F32) == entry) & (column % 8 == row % 8)
    picked = jnp.dot(hot.astype(F32).astype(BF), db_ref[...], preferred_element_type=F32)
    served[...] = picked.astype(BF).reshape(32, 16, 896)

    def reply(source, target):
        return remote(served.at[target], replies.at[source], as_.at[target], ar.at[source], target, z)

    loop(1, 32, lambda i: reply(dp, lax.rem(dp + i, 32)).start())
    r = lax.broadcasted_iota(jnp.int32, (192, 24), 0)
    request = lax.broadcasted_iota(jnp.int32, (192, 24), 1) == 12 * ((r // 8) % 2) + r // 16
    spread = jnp.dot(request.astype(F32).astype(BF), placed.astype(F32).astype(BF), preferred_element_type=F32)
    widen = (lax.broadcasted_iota(jnp.int32, (128, 512), 1) // 8
             == lax.broadcasted_iota(jnp.int32, (128, 512), 0))
    spread = jnp.dot(spread.astype(BF), widen.astype(F32).astype(BF), preferred_element_type=F32)
    token = (lax.broadcasted_iota(jnp.int32, (192, 512), 0) % 8
             == lax.broadcasted_iota(jnp.int32, (192, 512), 1) % 8)
    sel = jnp.where(token, spread, 0.0).astype(BF)
    slots(PACE["fetch"])
    replies[dp] = served[dp]
    loop(1, 32, lambda i: reply(lax.rem(dp + i, 32), dp).wait_recv())
    got = jnp.dot(sel, replies[...].reshape(512, 896), preferred_element_type=F32)
    mine[...] = got.astype(BF).reshape(12, 16, 896)

    def n_copy(k):
        p = plane_of(j, k)
        return p, remote(mine.at[k], near.at[slot_of(j, p), z], ns.at[k], nr.at[z], dp, p)

    def n_local(k):
        return pltpu.make_async_copy(mine.at[k], near.at[slot_of(j, z), z], lsem.at[2])

    def n_send(k):
        p, copy = n_copy(k)

        @pl.when(p == z)
        def _():
            n_local(k).start()

        @pl.when(p != z)
        def _():
            copy.start()

    loop(0, 12, n_send)
    slots(PACE["move"])

    def q2(source, target):
        return remote(qa.at[:, target], q6.at[slot_of(source, z)], q2s.at[target], q2r.at[source],
                      dp_of(x, target), z)

    def q2_local():
        return pltpu.make_async_copy(qa.at[:, j], q6.at[slot_of(j, z)], lsem.at[3])

    @pl.when(has_span(j, z))
    def _():
        q_local(0).wait()
        loop(1, 16, lambda i: remote(q_ref.at[0], qa.at[0, 0], qs.at[0], qr.at[lax.rem(z + i, 16)],
                                     dp, z).wait_recv())
        q2_local().start()
        loop(1, 8, lambda i: q2(j, lax.rem(j + i, 8)).start())


    def view(block, part):
        return near.at[slot_of(block, z), pl.ds(part * 8, 8)]

    def good(block):
        return has_span(block, z)

    @pl.when(good(j))
    def _():
        n_local(0).wait()
        loop(1, 16, lambda i: remote(mine.at[0], near.at[0, 0], ns.at[0], nr.at[lax.rem(z + i, 16)],
                                     dp, z).wait_recv())

    for part in (0, 1):
        gather_yc(view, here, gs, gr, good, part)
    slots(PACE["near"])
    forward, finish = gather_yc(view, here, gs, gr, good, None, lambda: slots(PACE["near_step"]))
    forward()
    finish()

    @pl.when(has_span(j, z))
    def _():
        q2_local().wait()
        loop(1, 8, lambda i: q2(j, lax.rem(j + i, 8)).wait_send())

    def q2_wait(i):
        other = lax.rem(j + i, 8)

        @pl.when(has_span(other, z))
        def _():
            q2(other, j).wait_recv()

    loop(1, 8, q2_wait)

    def w_land(i):
        for h in (0, 1):
            wf(h, i, 0).wait_recv()

    loop(0, NKV, w_land)

    scale = 1.0 / math.sqrt(128)

    def span(n):
        rows = near[n].reshape(256, 896)
        for h in (0, 1):
            keys = jnp.dot(rows, wall[h, 0:896, :], preferred_element_type=F32).astype(BF)
            values = jnp.dot(rows, wall[h, 896:1792, :], preferred_element_type=F32).astype(BF)
            for m in (0, 1):
                cut = slice(128 * m, 128 * m + 128)
                scores = lax.dot_general(q6[n, h, :, cut], keys[:, cut], (((1,), (1,)), ((), ())),
                                         preferred_element_type=F32) * scale
                w = jnp.exp(scores - jnp.max(scores, axis=-1, keepdims=True))
                w = w / jnp.sum(w, axis=-1, keepdims=True)
                o = jnp.dot(w.astype(BF), values[:, cut], preferred_element_type=F32)
                att[j, n, :, 256 * h + 128 * m:256 * h + 128 * m + 128] = o.astype(BF)

    def att_view(block, part):
        return att.at[block, pl.ds(3 * part, 3)]

    def always(block):
        return block >= 0

    for part in (0, 1):
        loop(3 * part, 3 * part + 3, span)
        slots(PACE["span"])
        gather_yc(att_view, here, ts, tr, always, part)
    forward, finish = gather_yc(att_view, here, ts, tr, always, None, lambda: slots(PACE["att_step"]))
    forward()
    slots(LAST)
    finish()
    loop(NKV, NP, w_land)

    def b_copy(g, source, target):
        return remote(res.at[g, slot_of(target, z)], ob.at[g, source], bs.at[g, target], br.at[g, source],
                      dp_of(x, target), z)

    for g in (0, 1):
        acc[...] = jnp.zeros_like(acc)

        def project(b):
            rows = att[b].reshape(384, 512)
            total = acc[...]
            for h in (0, 1):
                first = pl.multiple_of(2048 + (b + 8 * h) * 256, 256)
                total = total + jnp.dot(rows[:, 256 * h:256 * h + 256], wall[g, pl.ds(first, 256), :],
                                        preferred_element_type=F32)
            acc[...] = total

        loop(0, 8, project)
        res[g] = acc[...].astype(BF).reshape(6, 64, 256)

        def b_send(i):
            other = lax.rem(j + i, 8)

            @pl.when(has_span(other, z))
            def _():
                b_copy(g, j, other).start()

        loop(1, 8, b_send)

    def c_local(g, source, k):
        return pltpu.make_async_copy(ob.at[g, source], fb.at[k], lsem.at[0])

    def c_send(g, source):
        to = source + 8 * g
        k = span_of(j, z)

        @pl.when(to == z)
        def _():
            c_local(g, source, k).start()

        @pl.when(to != z)
        def _():
            remote(ob.at[g, source], fb.at[k], cs.at[to], cr.at[k], dp, to).start()

    @pl.when(has_span(j, z))
    def _():
        for g in (0, 1):
            ob[g, j] = res[g, slot_of(j, z)]
            c_send(g, j)

            def relay(i):
                other = lax.rem(j + i, 8)
                b_copy(g, other, j).wait_recv()
                c_send(g, other)

            loop(1, 8, relay)
        c_local(0, 0, 0).wait()

    load_hid.wait()

    def land(k):
        @pl.when(plane_of(j, k) != z)
        def _():
            remote(ob.at[0, 0], fb.at[k], cs.at[0], cr.at[k], dp, z).wait_recv()

        out_ref[k] = (hid_ref[k].astype(F32) + fb[k].astype(F32)).astype(BF)

    loop(0, 12, land)

    def sent(k):
        p, copy = n_copy(k)
        _, copy_q = q_copy(k)

        @pl.when(p != z)
        def _():
            copy.wait_send()
            copy_q.wait_send()

    loop(0, 12, sent)

    def sent_dp(i):
        other = lax.rem(dp + i, 32)
        req_copy(dp, other).wait_send()
        reply(dp, other).wait_send()

    loop(1, 32, sent_dp)

    def sent_w(i):
        wz(s, i, right, 0).wait_send()

        @pl.when(e == 0)
        def _():
            wz(s, i, left, 1).wait_send()

        @pl.when(e >= 2)
        def _():
            wz(1 - s, i, left, 1).wait_send()

        for h in (0, 1):
            wx(h, i, 0).wait_send()
            wx(h, i, 1).wait_send()
            wf(h, i, 0).wait_send()

    loop(0, NP, sent_w)

    def b_sent(i):
        other = lax.rem(j + i, 8)

        @pl.when(has_span(other, z))
        def _():
            b_copy(0, j, other).wait_send()
            b_copy(1, j, other).wait_send()

    loop(1, 8, b_sent)

    @pl.when(has_span(j, z))
    def _():
        def c_sent(i):
            to = lax.rem(z + i, 16)
            remote(ob.at[0, 0], fb.at[0], cs.at[to], cr.at[0], dp, to).wait_send()

        loop(1, 16, c_sent)


def layer(owners, slots, db, queries, w_key, w_value, w_out, hidden):
    dma = pltpu.SemaphoreType.DMA
    any_ = pl.BlockSpec(memory_space=pl.ANY)
    vmem = pl.BlockSpec(memory_space=pltpu.VMEM)
    return pl.pallas_call(
        layer_kernel,
        name="layer",
        out_shape=jax.ShapeDtypeStruct((12, 64, 256), BF),
        in_specs=[vmem, vmem, any_, any_, any_, any_, any_, any_],
        out_specs=vmem,
        scratch_shapes=[
            pltpu.VMEM((256, 896), BF),
            pltpu.VMEM((12, 64, 256), BF),
            pltpu.VMEM((8, 128), jnp.int32),
            pltpu.VMEM((2, 8, 64, 256), BF),
            pltpu.VMEM((6, 2, 64, 256), BF),
            pltpu.VMEM((32, 8, 128), jnp.int32),
            pltpu.VMEM((32, 16, 896), BF),
            pltpu.VMEM((32, 16, 896), BF),
            pltpu.VMEM((12, 16, 896), BF),
            pltpu.VMEM((6, 16, 16, 896), BF),
            pltpu.VMEM((2, NP * 4 * PIECE, 256), BF),
            pltpu.VMEM((8, 6, 64, 512), BF),
            pltpu.VMEM((384, 256), F32),
            pltpu.VMEM((2, 6, 64, 256), BF),
            pltpu.VMEM((2, 8, 64, 256), BF),
            pltpu.VMEM((12, 64, 256), BF),
            dma((32,)), dma((32,)),
            dma((12,)), dma((16,)),
            dma((8,)), dma((8,)),
            dma((32,)), dma((32,)),
            dma((12,)), dma((16,)),
            dma((7, 2)), dma((8, 2)),
            dma((NP,)),
            dma((2, NP)), dma((2, NP)),
            dma((2, 2, NP)), dma((2, 2, NP)),
            dma((2, NP)), dma((2, NP)),
            dma((7, 2)), dma((8, 2)),
            dma((2, 8)), dma((2, 8)),
            dma((16,)), dma((12,)),
            dma((4,)), dma((2,)),
        ],
        compiler_params=pltpu.CompilerParams(
            collective_id=0, has_side_effects=True, vmem_limit_bytes=62 * 2**20
        ),
    )(owners, slots, db, queries, w_key, w_value, w_out, hidden)


def per_device(hidden, queries, database, w_key, w_value, w_out, owners, entry_slots):
    mixed = layer(
        owners.T, entry_slots.T, database.reshape(256, 896), queries.reshape(12, 64, 256),
        w_key, w_value, w_out, hidden.reshape(12, 64, 256),
    )
    return mixed.reshape(768, 256)


def solution(mesh):
    in_specs = (
        P("dp", "tensor"),
        P("dp", "tensor"),
        P("dp", "tensor", None),
        P(None, "tensor"),
        P(None, "tensor"),
        P(None, "tensor"),
        P("dp", None),
        P("dp", None),
    )
    return jax.shard_map(
        per_device, mesh=mesh, in_specs=in_specs, out_specs=P("dp", "tensor"), check_vma=False
    )
```

time: 201 us -> 165 us (0.82)
  the two profiles are of different devices: /device:TPU:79 before, /device:TPU:1 now
where the time goes in v2:
time: 165 us
  Pallas kernels  163 us (99%)
  local copies, waits for them, and re-layouts  1.77 us (1%)
    pallas_call x1, Pallas kernels, layer(): pl.pallas_call(layer_kernel, name='layer', out_shape=jax.ShapeDtypeStruct...  163 us

profile of v2, /device:TPU:1, one launch (start us, length us, event | category | flops | bytes accessed | tf_op | source)
XLA Modules:
  0.0 164.8 jit_solution(11816436786977680298)
XLA Ops:
  0.0 163.0 %layer.1 = bf16[12,64,256]{2,1,0:T(8,128)(2,1)} custom-call(s32[2,12]{1,0:T(2,128)} %bitcast.10, s32[2,12]{1,0:T(2,128)} %bitcast.11, bf16[256,896]{1,0:T(8,128)(2,1)} %bitcast.7, bf16[12,64,256]{2,1,0:T(8,128)(2,1)} %bitcast.8, bf16[896,256]{1,0:T(8,128)(2,1)} %wk_ref.1, bf16[896,256]{1,0:T(8,128)(2,1)} %wv_ref.1, bf16[4096,256]{1,0:T(8,128)(2,1)} %wo_ref.1, ...), custom_call_target="tpu_custom_call" | custom-call | tf_op jit(solution)/shard_map/layer/pallas_call | solution.py:595
  163.0 1.8 %copy.10 = bf16[768,256]{1,0:T(8,128)(2,1)} copy(bf16[768,256]{1,0:T(8,128)(2,1)} %bitcast.6) | data formatting | bytes 786432

commit v3 on v2

--- a/solution.py
+++ b/solution.py
@@ -149,7 +149,7 @@
 
 
 def layer_kernel(own_ref, ent_ref, db_hbm, q_ref, wk_ref, wv_ref, wo_ref, hid_hbm, out_ref,
-                 db_ref, hid_ref, req_ref, qa, q6, rall, served, replies, mine, near, wall, att, acc, res, ob, fb,
+                 db_ref, hid_ref, req_ref, qa, q6, rall, served, replies, mine, near, wall, att, res, ob, fb,
                  rs, rr, qs, qr, q2s, q2r, as_, ar, ns, nr, gs, gr,
                  wl, zs, zr, xs, xr, fs, fr, ts, tr, bs, br, cs, cr, lsem, load):
     here = where_am_i()
@@ -186,7 +186,7 @@
                 own(i, wv_ref, jnp.clip(g - 7, 0, 6)).start()
 
         for i in range(NKV, NP):
-            own(i, wo_ref, 4 * (i - NKV) + x).start()
+            own(i, wo_ref, 2 * (i - NKV) + 16 * (x // 2) + lax.rem(x, 2)).start()
 
     load_hid.start()
     barrier = pltpu.get_barrier_semaphore()
@@ -470,19 +470,15 @@
                       dp_of(x, target), z)
 
     for g in (0, 1):
-        acc[...] = jnp.zeros_like(acc)
-
-        def project(b):
-            rows = att[b].reshape(384, 512)
-            total = acc[...]
-            for h in (0, 1):
-                first = pl.multiple_of(2048 + (b + 8 * h) * 256, 256)
-                total = total + jnp.dot(rows[:, 256 * h:256 * h + 256], wall[g, pl.ds(first, 256), :],
-                                        preferred_element_type=F32)
-            acc[...] = total
-
-        loop(0, 8, project)
-        res[g] = acc[...].astype(BF).reshape(6, 64, 256)
+        def project(n):
+            total = None
+            for b in range(8):
+                rows = att[b, pl.ds(3 * n, 3)].reshape(192, 512)
+                part = jnp.dot(rows, wall[g, 2048 + 512 * b:2560 + 512 * b, :], preferred_element_type=F32)
+                total = part if total is None else total + part
+            res[g, pl.ds(3 * n, 3)] = total.astype(BF).reshape(3, 64, 256)
+
+        loop(0, 2, project)
 
         def b_send(i):
             other = lax.rem(j + i, 8)
@@ -611,7 +607,6 @@
             pltpu.VMEM((6, 16, 16, 896), BF),
             pltpu.VMEM((2, NP * 4 * PIECE, 256), BF),
             pltpu.VMEM((8, 6, 64, 512), BF),
-            pltpu.VMEM((384, 256), F32),
             pltpu.VMEM((2, 6, 64, 256), BF),
             pltpu.VMEM((2, 8, 64, 256), BF),
             pltpu.VMEM((12, 64, 256), BF),

time: 165 us -> 164 us (level)
  no operation moved by 1% of the time
where the time goes in v3:
time: 164 us
  Pallas kernels  162 us (99%)
  local copies, waits for them, and re-layouts  1.77 us (1%)
    pallas_call x1, Pallas kernels, layer(): pl.pallas_call(layer_kernel, name='layer', out_shape=jax.ShapeDtypeStruct...  162 us

profile of v3, /device:TPU:1, one launch (start us, length us, event | category | flops | bytes accessed | tf_op | source)
XLA Modules:
  0.0 164.2 jit_solution(8927641191688893638)
XLA Ops:
  0.0 162.5 %layer.1 = bf16[12,64,256]{2,1,0:T(8,128)(2,1)} custom-call(s32[2,12]{1,0:T(2,128)} %bitcast.10, s32[2,12]{1,0:T(2,128)} %bitcast.11, bf16[256,896]{1,0:T(8,128)(2,1)} %bitcast.7, bf16[12,64,256]{2,1,0:T(8,128)(2,1)} %bitcast.8, bf16[896,256]{1,0:T(8,128)(2,1)} %wk_ref.1, bf16[896,256]{1,0:T(8,128)(2,1)} %wv_ref.1, bf16[4096,256]{1,0:T(8,128)(2,1)} %wo_ref.1, ...), custom_call_target="tpu_custom_call" | custom-call | tf_op jit(solution)/shard_map/layer/pallas_call | solution.py:591
  162.5 1.8 %copy.10 = bf16[768,256]{1,0:T(8,128)(2,1)} copy(bf16[768,256]{1,0:T(8,128)(2,1)} %bitcast.6) | data formatting | bytes 786432

commit v4 on v3

--- a/solution.py
+++ b/solution.py
@@ -395,18 +395,22 @@
 
 
     def view(block, part):
-        return near.at[slot_of(block, z), pl.ds(part * 8, 8)]
+        return near.at[slot_of(block, z), pl.ds(8 * lax.rem(part + z // 8, 2), 8)]
 
     def good(block):
         return has_span(block, z)
 
-    @pl.when(good(j))
-    def _():
-        n_local(0).wait()
-        loop(1, 16, lambda i: remote(mine.at[0], near.at[0, 0], ns.at[0], nr.at[lax.rem(z + i, 16)],
-                                     dp, z).wait_recv())
+    def n_land(source):
+        remote(mine.at[0], near.at[0, 0], ns.at[0], nr.at[source], dp, z).wait_recv()
 
     for part in (0, 1):
+        @pl.when(good(j))
+        def _():
+            half = 8 * lax.rem(part + z // 8, 2)
+            if part == 0:
+                n_local(0).wait()
+            loop(1 - part, 8, lambda i: n_land(half + lax.rem(z + i, 8)))
+
         gather_yc(view, here, gs, gr, good, part)
     slots(PACE["near"])
     forward, finish = gather_yc(view, here, gs, gr, good, None, lambda: slots(PACE["near_step"]))

time: 164 us -> 164 us (level)
  no operation moved by 1% of the time
where the time goes in v4:
time: 164 us
  Pallas kernels  162 us (99%)
  local copies, waits for them, and re-layouts  1.77 us (1%)
    pallas_call x1, Pallas kernels, layer(): pl.pallas_call(layer_kernel, name='layer', out_shape=jax.ShapeDtypeStruct...  162 us

profile of v4, /device:TPU:1, one launch (start us, length us, event | category | flops | bytes accessed | tf_op | source)
XLA Modules:
  0.0 164.3 jit_solution(5978131980994841712)
XLA Ops:
  0.0 162.5 %layer.1 = bf16[12,64,256]{2,1,0:T(8,128)(2,1)} custom-call(s32[2,12]{1,0:T(2,128)} %bitcast.10, s32[2,12]{1,0:T(2,128)} %bitcast.11, bf16[256,896]{1,0:T(8,128)(2,1)} %bitcast.7, bf16[12,64,256]{2,1,0:T(8,128)(2,1)} %bitcast.8, bf16[896,256]{1,0:T(8,128)(2,1)} %wk_ref.1, bf16[896,256]{1,0:T(8,128)(2,1)} %wv_ref.1, bf16[4096,256]{1,0:T(8,128)(2,1)} %wo_ref.1, ...), custom_call_target="tpu_custom_call" | custom-call | tf_op jit(solution)/shard_map/layer/pallas_call | solution.py:595
  162.5 1.8 %copy.10 = bf16[768,256]{1,0:T(8,128)(2,1)} copy(bf16[768,256]{1,0:T(8,128)(2,1)} %bitcast.6) | data formatting | bytes 786432
